TPU v7x, 32 devices: a whole 2x2x4 slice. The times are simulated.
32 devices in a mesh: ctx: 16 (over z, y, core), tp: 2 (over x).
Axes of the slice: x: 2, y: 2, z: 4, core: 2. Of those that a mesh axis runs over, the one named last changes fastest.
Arguments:
- activations: bfloat16 [2048, 4096], P(('ctx', 'tp')), may hold values from -24 to 24
- query_weight: bfloat16 [4096, 4096], P(None, 'tp'), may hold values from -0.09375 to 0.09375
- key_weight: bfloat16 [4096, 1024], P(None, 'tp'), may hold values from -0.09375 to 0.09375
- value_weight: bfloat16 [4096, 1024], P(None, 'tp'), may hold values from -0.09375 to 0.09375
Outputs:
- attended: bfloat16 [2048, 4096], P('ctx', 'tp')
All inputs are finite; a program needn't handle non-finite values.
Results may differ from a plain program's by a relative error of at most 0.012.
The roundings to bfloat16 on the way count: a program that leaves them out, or rounds other values in their place, can miss the bound.
Values may be sent and summed in bfloat16 or wider, within the bound.
No kernel may reach another device: no remote copies, remote signals or barrier semaphores. Data moves between devices by JAX's collectives and lax.ppermute only.
A program may use at most 128 MiB of HBM per device.

v0:
```python
import math
import jax
import jax.numpy as jnp
from jax import lax
from jax.sharding import PartitionSpec as P

HD = 128
THETA = 500000.0
NEGATIVE = -1e30


def rotate(heads_in, positions):
    width = heads_in.shape[-1]
    half_width = width // 2
    frequency = THETA ** (-(jnp.arange(half_width).astype(jnp.float32) * 2.0 / width))
    angles = positions[:, None] * frequency[None, :]
    cosine = jnp.cos(angles)[:, None, :]
    sine_table = jnp.sin(angles)[:, None, :]
    front_half = heads_in[..., :half_width]
    back_half = heads_in[..., half_width:]
    return jnp.concatenate(
        [
            front_half * cosine - back_half * sine_table,
            back_half * cosine + front_half * sine_table,
        ],
        axis=-1,
    )


def block_update(state, query_block, query_pos, key_block, value_block, key_pos):
    row_top, totals, accum = state
    scale = 1.0 / math.sqrt(query_block.shape[-1])
    scores = (
        lax.dot_general(
            query_block, key_block, (((1,), (1,)), ((), ())), preferred_element_type=jnp.float32
        )
        * scale
    )
    allowed = key_pos[None, :] <= query_pos[:, None]
    block_top = jnp.max(jnp.where(allowed, scores, NEGATIVE), axis=1)
    new_top = jnp.maximum(row_top, block_top)
    correction = jnp.exp(row_top - new_top)
    weights = jnp.where(allowed, jnp.exp(scores - new_top[:, None]), 0.0)
    totals = totals * correction + jnp.sum(weights, axis=1)
    accum = accum * correction[:, None] + jnp.dot(
        weights.astype(jnp.bfloat16), value_block, preferred_element_type=jnp.float32
    )
    return (new_top, totals, accum)


def attend(groups, keys, values):
    carry_start = []
    for query_rows, query_pos, kv_slot, query_step in groups:
        row_count = query_rows.shape[0]
        blocks_count = row_count // query_step
        carry_start.append(
            (
                jnp.full((blocks_count, query_step), NEGATIVE, jnp.float32),
                jnp.zeros((blocks_count, query_step), jnp.float32),
                jnp.zeros((blocks_count, query_step, HD), jnp.float32),
            )
        )
    carry = tuple(carry_start)
    key_piece = lax.all_gather(keys, "ctx", axis=0, tiled=True)
    value_piece = lax.all_gather(values, "ctx", axis=0, tiled=True)
    piece_rows = key_piece.shape[0]
    key_step = math.gcd(piece_rows, 512)
    updated = []
    for (query_rows, query_pos, kv_slot, query_step), fold_state in zip(groups, carry):
        key_chosen = lax.dynamic_index_in_dim(
            key_piece.reshape(piece_rows, -1, HD), kv_slot, 1, keepdims=False
        )
        value_chosen = lax.dynamic_index_in_dim(
            value_piece.reshape(piece_rows, -1, HD), kv_slot, 1, keepdims=False
        )
        key_blocks = key_chosen.reshape(piece_rows // key_step, key_step, HD)
        value_blocks = value_chosen.reshape(piece_rows // key_step, key_step, HD)
        block_starts = jnp.arange(piece_rows // key_step, dtype=jnp.int32) * key_step
        blocks_count = fold_state[0].shape[0]
        query_blocks = query_rows.reshape(blocks_count, query_step, HD)
        pos_blocks = query_pos.reshape(blocks_count, query_step)

        def per_query(items):
            query_block, pos_block, row_top, totals, accum = items
            last_pos = jnp.max(pos_block)

            def per_key(inner, key_items):
                key_block, value_block, key_start = key_items
                key_pos = key_start + jnp.arange(key_step, dtype=jnp.int32)
                result = lax.cond(
                    key_start <= last_pos,
                    lambda current: block_update(
                        current, query_block, pos_block, key_block, value_block, key_pos
                    ),
                    lambda current: current,
                    inner,
                )
                return (result, None)

            final, unused = lax.scan(
                per_key, (row_top, totals, accum), (key_blocks, value_blocks, block_starts)
            )
            return final

        updated.append(
            lax.map(
                per_query, (query_blocks, pos_blocks, fold_state[0], fold_state[1], fold_state[2])
            )
        )
    final_state = tuple(updated)
    results = []
    for state in final_state:
        outcome = state[2] / state[1][..., None]
        results.append(outcome.reshape(-1, HD))
    return results


def local(activations, query_weight, key_weight, value_weight):
    tensor_count = lax.axis_size("tp")
    context_index = lax.axis_index("ctx")
    local_rows = activations.shape[0] * tensor_count
    heads_here = query_weight.shape[1] // HD
    kv_here = key_weight.shape[1] // HD
    group = heads_here // kv_here
    query_width = heads_here * HD
    key_width = kv_here * HD
    gathered = lax.all_gather(activations, "tp", axis=0, tiled=True)
    projected = jnp.concatenate(
        [
            jnp.dot(gathered, query_weight, preferred_element_type=jnp.float32),
            jnp.dot(gathered, key_weight, preferred_element_type=jnp.float32),
            jnp.dot(gathered, value_weight, preferred_element_type=jnp.float32),
        ],
        axis=1,
    )
    token_pos = context_index * local_rows + jnp.arange(local_rows, dtype=jnp.int32)
    positions = token_pos.astype(jnp.float32)
    queries = rotate(
        projected[:, :query_width].reshape(local_rows, heads_here, HD), positions
    ).astype(jnp.bfloat16)
    keys = (
        rotate(
            projected[:, query_width : query_width + key_width].reshape(local_rows, kv_here, HD),
            positions,
        )
        .astype(jnp.bfloat16)
        .reshape(local_rows, key_width)
    )
    values = projected[:, query_width + key_width :].astype(jnp.bfloat16)
    groups = []
    for kv_slot in range(kv_here):
        chosen = queries[:, kv_slot * group : (kv_slot + 1) * group].reshape(local_rows * group, HD)
        groups.append(
            (chosen, jnp.repeat(token_pos, group), kv_slot, math.gcd(local_rows * group, 512))
        )
    results = attend(groups, keys, values)
    pieces = [outcome.astype(jnp.bfloat16).reshape(local_rows, group * HD) for outcome in results]
    return jnp.concatenate(pieces, axis=1)


def solution(mesh):
    in_specs = (P(("ctx", "tp"), None), P(None, "tp"), P(None, "tp"), P(None, "tp"))
    out_specs = P("ctx", "tp")
    return jax.shard_map(local, mesh=mesh, in_specs=in_specs, out_specs=out_specs, check_vma=False)
```

profile of v0, /device:TPU:25, one launch (start us, length us, event | category | flops | bytes accessed | tf_op | source)
XLA Modules:
  0.0 219.5 jit_solution(12466268835597819170)
XLA Ops:
  7.6 23.6 %all-gather.4.cloned.1.call-done = bf16[128,4096]{1,0:T(8,128)(2,1)} async-done(((bf16[64,4096]{1,0:T(8,128)(2,1)}), bf16[128,4096]{1,0:T(8,128)(2,1)}) %all-gather.4.cloned.1.call-update) | async-done | bytes 1048592 | tf_op jit(solution)/shard_map/all_gather | solution.py:127
  31.2 3.3 %fusion.78 = f32[128,512]{1,0:T(8,128)S(1)} fusion(bf16[128,4096]{1,0:T(8,128)(2,1)} %all-gather.4.cloned.1.call-done, bf16[4096,512]{1,0:T(8,128)(2,1)} %param.22), kind=kOutput, calls=%fused_computation.123 | convolution fusion | flops 536870912 | bytes 5505024 | tf_op jit(solution)/shard_map/dot_general | solution.py:131
  36.0 3.6 %convolution_convert_fusion = bf16[128,512]{1,0:T(8,128)(2,1)} fusion(bf16[128,4096]{1,0:T(8,128)(2,1)S(1)} %copy-done, bf16[4096,512]{1,0:T(8,128)(2,1)} %param.23), kind=kOutput, calls=%fused_computation.93 | convolution fusion | flops 536936448 | bytes 5373952 | tf_op jit(solution)/shard_map/dot_general | solution.py:132
  40.3 8.2 %convolution_bitcast_fusion = f32[16,8,16,128]{3,1,2,0:T(8,128)S(1)} fusion(bf16[128,4096]{1,0:T(8,128)(2,1)S(1)} %copy-done, bf16[4096,2048]{1,0:T(8,128)(2,1)} %param.21), kind=kOutput, calls=%fused_computation.92 | convolution fusion | flops 2147483648 | bytes 18874368 | tf_op jit(solution)/shard_map/dot_general | solution.py:130
  49.3 1.3 fusion.73
  50.6 25.6 %all-gather.6.cloned.1.call-done = bf16[2048,512]{0,1:T(8,128)(2,1)} async-done(((bf16[128,512]{0,1:T(8,128)(2,1)}), bf16[2048,512]{0,1:T(8,128)(2,1)}) %all-gather.6.cloned.1.call-update) | async-done | bytes 2097168 | tf_op jit(solution)/shard_map/all_gather | solution.py:64
  76.1 2.7 %fusion.77 = (bf16[2048,1,128]{0,2,1:T(8,128)(2,1)S(1)}, bf16[2048,1,128]{0,2,1:T(8,128)(2,1)}, bf16[2048,1,128]{0,2,1:T(8,128)(2,1)}, bf16[2048,1,128]{0,2,1:T(8,128)(2,1)}) fusion(bf16[2048,4,128]{0,2,1:T(8,128)(2,1)} %bitcast.80), kind=kLoop, calls=%fused_computation.122 | loop fusion | bytes 4194304 | tf_op jit(solution)/shard_map/jit(dynamic_index_in_dim)/dynamic_slice | solution.py:70
  79.9 39.1 %all-gather.8.cloned.1.call-done = bf16[2048,512]{1,0:T(8,128)(2,1)} async-done(((bf16[128,512]{1,0:T(8,128)(2,1)}), bf16[2048,512]{1,0:T(8,128)(2,1)}) %all-gather.8.cloned.1.call-update) | async-done | bytes 2097168 | tf_op jit(solution)/shard_map/all_gather | solution.py:65
  119.0 2.5 %reshape.177 = bf16[2048,4,128]{2,1,0:T(4,128)(2,1)S(1)} reshape(bf16[2048,512]{1,0:T(8,128)(2,1)} %all-gather.8.cloned.1.call-done) | data formatting | bytes 4194304 | tf_op jit(solution)/shard_map/reshape | solution.py:74
  121.5 4.0 %fusion.76 = (bf16[2048,1,128]{2,1,0:T(2,128)(2,1)S(1)}, bf16[2048,1,128]{2,1,0:T(2,128)(2,1)}, bf16[2048,1,128]{2,1,0:T(2,128)(2,1)}, bf16[2048,1,128]{2,1,0:T(2,128)(2,1)S(1)}) fusion(bf16[2048,4,128]{2,1,0:T(4,128)(2,1)S(1)} %reshape.177), kind=kLoop, calls=%fused_computation.121 | loop fusion | bytes 4194304 | tf_op jit(solution)/shard_map/jit(dynamic_index_in_dim)/dynamic_slice | solution.py:73
  126.5 22.5 %while.96 = (s32[]{:T(128)}, f32[512]{0:T(512)S(1)}, f32[512]{0:T(512)S(1)}, f32[512,128]{1,0:T(8,128)S(1)}, s32[4]{0:T(128)S(1)}, /*index=5*/s32[]{:T(128)}, bf...) while((s32[]{:T(128)}, f32[512]{0:T(512)S(1)}, ...), condition=%wide.region_6.7_spmd.clone, body=%wide.region_1.0_spmd.clone.sunk | while | flops 137496064 | bytes 4122387 | solution.py:100
  128.3 3.8 %conditional.12 = ((f32[512]{0:T(512)S(1)}, f32[512]{0:T(512)S(1)}, f32[512,128]{1,0:T(8,128)S(1)})) conditional(s32[]{:T(128)} %convert_element_type.119, (f32[512]{0:T(512)S(1)}, f32[512]{0:T(512)S(1)}, f32[512,128]{1,0:T(8,128)S(1)}) %tuple.163, (s32[]{:T(128)}, s32[512]{0:T(512)S(1)}, s32[128]{0:T(128)S(1)}, bf16[4,512,128]{2,1,0:T(8,128)(2,1)}, ...), branch_computations={%region_2.2_spmd, %region_3.5_spmd} | conditional | flops 137496064 | bytes 4120100 | solution.py:90
  129.1 1.3 fusion.9
  130.7 1.4 convolution_add_fusion
  133.9 3.8 %conditional.12 = ((f32[512]{0:T(512)S(1)}, f32[512]{0:T(512)S(1)}, f32[512,128]{1,0:T(8,128)S(1)})) conditional(s32[]{:T(128)} %convert_element_type.119, (f32[512]{0:T(512)S(1)}, f32[512]{0:T(512)S(1)}, f32[512,128]{1,0:T(8,128)S(1)}) %tuple.163, (s32[]{:T(128)}, s32[512]{0:T(512)S(1)}, s32[128]{0:T(128)S(1)}, bf16[4,512,128]{2,1,0:T(8,128)(2,1)}, ...), branch_computations={%region_2.2_spmd, %region_3.5_spmd} | conditional | flops 137496064 | bytes 4120100 | solution.py:90
  134.7 1.3 fusion.9
  136.3 1.4 convolution_add_fusion
  139.5 3.8 %conditional.12 = ((f32[512]{0:T(512)S(1)}, f32[512]{0:T(512)S(1)}, f32[512,128]{1,0:T(8,128)S(1)})) conditional(s32[]{:T(128)} %convert_element_type.119, (f32[512]{0:T(512)S(1)}, f32[512]{0:T(512)S(1)}, f32[512,128]{1,0:T(8,128)S(1)}) %tuple.163, (s32[]{:T(128)}, s32[512]{0:T(512)S(1)}, s32[128]{0:T(128)S(1)}, bf16[4,512,128]{2,1,0:T(8,128)(2,1)}, ...), branch_computations={%region_2.2_spmd, %region_3.5_spmd} | conditional | flops 137496064 | bytes 4120100 | solution.py:90
  140.3 1.3 fusion.9
  141.9 1.4 convolution_add_fusion
  145.2 3.8 %conditional.12 = ((f32[512]{0:T(512)S(1)}, f32[512]{0:T(512)S(1)}, f32[512,128]{1,0:T(8,128)S(1)})) conditional(s32[]{:T(128)} %convert_element_type.119, (f32[512]{0:T(512)S(1)}, f32[512]{0:T(512)S(1)}, f32[512,128]{1,0:T(8,128)S(1)}) %tuple.163, (s32[]{:T(128)}, s32[512]{0:T(512)S(1)}, s32[128]{0:T(128)S(1)}, bf16[4,512,128]{2,1,0:T(8,128)(2,1)}, ...), branch_computations={%region_2.2_spmd, %region_3.5_spmd} | conditional | flops 137496064 | bytes 4120100 | solution.py:90
  145.9 1.3 fusion.9
  147.5 1.4 convolution_add_fusion
  151.2 23.1 %while.97 = (s32[]{:T(128)}, f32[512]{0:T(512)S(1)}, f32[512]{0:T(512)S(1)}, f32[512,128]{1,0:T(8,128)S(1)}, s32[4]{0:T(128)S(1)}, /*index=5*/s32[]{:T(128)}, bf...) while((s32[]{:T(128)}, f32[512]{0:T(512)S(1)}, ...), condition=%wide.region_12.13_spmd.clone, body=%wide.region_7.12_spmd.clone.sunk | while | flops 137496064 | bytes 4122387 | solution.py:100
  153.1 3.9 %conditional.13 = ((f32[512]{0:T(512)S(1)}, f32[512]{0:T(512)S(1)}, f32[512,128]{1,0:T(8,128)S(1)})) conditional(s32[]{:T(128)} %convert_element_type.120, (f32[512]{0:T(512)S(1)}, f32[512]{0:T(512)S(1)}, f32[512,128]{1,0:T(8,128)S(1)}) %tuple.166, (s32[]{:T(128)}, s32[512]{0:T(512)S(1)}, s32[128]{0:T(128)S(1)}, bf16[4,512,128]{2,1,0:T(8,128)(2,1)}, ...), branch_computations={%region_8.8_spmd, %region_9.11_spmd} | conditional | flops 137496064 | bytes 4120100 | solution.py:90
  153.9 1.3 fusion.25
  155.5 1.4 convolution_add_fusion.1
  158.9 3.9 %conditional.13 = ((f32[512]{0:T(512)S(1)}, f32[512]{0:T(512)S(1)}, f32[512,128]{1,0:T(8,128)S(1)})) conditional(s32[]{:T(128)} %convert_element_type.120, (f32[512]{0:T(512)S(1)}, f32[512]{0:T(512)S(1)}, f32[512,128]{1,0:T(8,128)S(1)}) %tuple.166, (s32[]{:T(128)}, s32[512]{0:T(512)S(1)}, s32[128]{0:T(128)S(1)}, bf16[4,512,128]{2,1,0:T(8,128)(2,1)}, ...), branch_computations={%region_8.8_spmd, %region_9.11_spmd} | conditional | flops 137496064 | bytes 4120100 | solution.py:90
  159.7 1.3 fusion.25
  161.3 1.4 convolution_add_fusion.1
  164.7 3.9 %conditional.13 = ((f32[512]{0:T(512)S(1)}, f32[512]{0:T(512)S(1)}, f32[512,128]{1,0:T(8,128)S(1)})) conditional(s32[]{:T(128)} %convert_element_type.120, (f32[512]{0:T(512)S(1)}, f32[512]{0:T(512)S(1)}, f32[512,128]{1,0:T(8,128)S(1)}) %tuple.166, (s32[]{:T(128)}, s32[512]{0:T(512)S(1)}, s32[128]{0:T(128)S(1)}, bf16[4,512,128]{2,1,0:T(8,128)(2,1)}, ...), branch_computations={%region_8.8_spmd, %region_9.11_spmd} | conditional | flops 137496064 | bytes 4120100 | solution.py:90
  165.5 1.3 fusion.25
  167.1 1.4 convolution_add_fusion.1
  170.4 3.9 %conditional.13 = ((f32[512]{0:T(512)S(1)}, f32[512]{0:T(512)S(1)}, f32[512,128]{1,0:T(8,128)S(1)})) conditional(s32[]{:T(128)} %convert_element_type.120, (f32[512]{0:T(512)S(1)}, f32[512]{0:T(512)S(1)}, f32[512,128]{1,0:T(8,128)S(1)}) %tuple.166, (s32[]{:T(128)}, s32[512]{0:T(512)S(1)}, s32[128]{0:T(128)S(1)}, bf16[4,512,128]{2,1,0:T(8,128)(2,1)}, ...), branch_computations={%region_8.8_spmd, %region_9.11_spmd} | conditional | flops 137496064 | bytes 4120100 | solution.py:90
  171.3 1.3 fusion.25
  172.9 1.4 convolution_add_fusion.1
  175.7 19.9 %while.98 = (s32[]{:T(128)}, f32[512]{0:T(512)S(1)}, f32[512]{0:T(512)S(1)}, f32[512,128]{1,0:T(8,128)S(1)}, s32[4]{0:T(128)S(1)}, /*index=5*/s32[]{:T(128)}, bf...) while((s32[]{:T(128)}, f32[512]{0:T(512)S(1)}, ...), condition=%wide.region_18.19_spmd.clone, body=%wide.region_13.18_spmd.clone.sunk | while | flops 137496064 | bytes 4121879 | solution.py:100
  177.8 2.9 %conditional.14 = ((f32[512]{0:T(512)S(1)}, f32[512]{0:T(512)S(1)}, f32[512,128]{1,0:T(8,128)S(1)})) conditional(s32[]{:T(128)} %convert_element_type.121, (f32[512]{0:T(512)S(1)}, f32[512]{0:T(512)S(1)}, f32[512,128]{1,0:T(8,128)S(1)}) %tuple.169, (s32[]{:T(128)}, s32[512]{0:T(512)S(1)}, s32[128]{0:T(128)S(1)}, bf16[4,512,128]{2,1,0:T(8,128)(2,1)}, ...), branch_computations={%region_14.14_spmd, %region_15.17_spmd} | conditional | flops 137496064 | bytes 4119592 | solution.py:90
  178.7 1.2 fusion.41
  182.7 2.9 %conditional.14 = ((f32[512]{0:T(512)S(1)}, f32[512]{0:T(512)S(1)}, f32[512,128]{1,0:T(8,128)S(1)})) conditional(s32[]{:T(128)} %convert_element_type.121, (f32[512]{0:T(512)S(1)}, f32[512]{0:T(512)S(1)}, f32[512,128]{1,0:T(8,128)S(1)}) %tuple.169, (s32[]{:T(128)}, s32[512]{0:T(512)S(1)}, s32[128]{0:T(128)S(1)}, bf16[4,512,128]{2,1,0:T(8,128)(2,1)}, ...), branch_computations={%region_14.14_spmd, %region_15.17_spmd} | conditional | flops 137496064 | bytes 4119592 | solution.py:90
  187.7 2.9 %conditional.14 = ((f32[512]{0:T(512)S(1)}, f32[512]{0:T(512)S(1)}, f32[512,128]{1,0:T(8,128)S(1)})) conditional(s32[]{:T(128)} %convert_element_type.121, (f32[512]{0:T(512)S(1)}, f32[512]{0:T(512)S(1)}, f32[512,128]{1,0:T(8,128)S(1)}) %tuple.169, (s32[]{:T(128)}, s32[512]{0:T(512)S(1)}, s32[128]{0:T(128)S(1)}, bf16[4,512,128]{2,1,0:T(8,128)(2,1)}, ...), branch_computations={%region_14.14_spmd, %region_15.17_spmd} | conditional | flops 137496064 | bytes 4119592 | solution.py:90
  188.6 1.2 fusion.41
  192.7 2.9 %conditional.14 = ((f32[512]{0:T(512)S(1)}, f32[512]{0:T(512)S(1)}, f32[512,128]{1,0:T(8,128)S(1)})) conditional(s32[]{:T(128)} %convert_element_type.121, (f32[512]{0:T(512)S(1)}, f32[512]{0:T(512)S(1)}, f32[512,128]{1,0:T(8,128)S(1)}) %tuple.169, (s32[]{:T(128)}, s32[512]{0:T(512)S(1)}, s32[128]{0:T(128)S(1)}, bf16[4,512,128]{2,1,0:T(8,128)(2,1)}, ...), branch_computations={%region_14.14_spmd, %region_15.17_spmd} | conditional | flops 137496064 | bytes 4119592 | solution.py:90
  196.3 15.6 %while.99 = (s32[]{:T(128)}, f32[512]{0:T(512)S(1)}, f32[512]{0:T(512)S(1)}, f32[512,128]{1,0:T(8,128)S(1)}, s32[4]{0:T(128)S(1)}, /*index=5*/s32[]{:T(128)}, bf...) while((s32[]{:T(128)}, f32[512]{0:T(512)S(1)}, ...), condition=%wide.region_24.25_spmd.clone, body=%wide.region_19.24_spmd.clone.sunk | while | flops 137496064 | bytes 4121371 | solution.py:100
  198.2 2.0 conditional.15
  202.1 2.0 conditional.15
  206.0 2.0 conditional.15
  209.9 2.0 conditional.15
  (216 shorter events, 46.2 us)
Async XLA Ops:
  6.5 24.7 %all-gather.4.cloned.1.call-start = ((), (), s32[]{:S(2)}) async-start(), calls=%async_computation | async-start | bytes 1572864 | tf_op jit(solution)/shard_map/all_gather | solution.py:127
  7.3 68.9 %all-gather.6.cloned.1.call-start = ((), (), s32[]{:S(2)}) async-start(), calls=%async_computation.1 | async-start | bytes 2228224 | tf_op jit(solution)/shard_map/all_gather | solution.py:64
  31.2 4.8 %copy-start = (bf16[128,4096]{1,0:T(8,128)(2,1)S(1)}, bf16[128,4096]{1,0:T(8,128)(2,1)}, u32[]{:S(2)}) copy-start(bf16[128,4096]{1,0:T(8,128)(2,1)} %all-gather.4.cloned.1.call-done) | copy-start | bytes 3145732
  35.9 83.1 %all-gather.8.cloned.1.call-start = ((), (), s32[]{:S(2)}) async-start(), calls=%async_computation.2 | async-start | bytes 2228224 | tf_op jit(solution)/shard_map/all_gather | solution.py:65
  126.5 22.7 %copy-start.5 = (bf16[2048,1,128]{0,2,1:T(8,128)(2,1)S(1)}, bf16[2048,1,128]{0,2,1:T(8,128)(2,1)}, u32[]{:S(2)}) copy-start(bf16[2048,1,128]{0,2,1:T(8,128)(2,1)} %get-tuple-element.984) | copy-start | bytes 1572868
  126.5 23.7 %copy-start.2 = (bf16[2048,1,128]{2,1,0:T(2,128)(2,1)S(1)}, bf16[2048,1,128]{2,1,0:T(2,128)(2,1)}, u32[]{:S(2)}) copy-start(bf16[2048,1,128]{2,1,0:T(2,128)(2,1)} %get-tuple-element.979) | copy-start | bytes 1572868
  151.2 23.4 %copy-start.4 = (bf16[2048,1,128]{0,2,1:T(8,128)(2,1)S(1)}, bf16[2048,1,128]{0,2,1:T(8,128)(2,1)}, u32[]{:S(2)}) copy-start(bf16[2048,1,128]{0,2,1:T(8,128)(2,1)} %get-tuple-element.983) | copy-start | bytes 1572868
  151.2 24.4 %copy-start.1 = (bf16[2048,1,128]{2,1,0:T(2,128)(2,1)S(1)}, bf16[2048,1,128]{2,1,0:T(2,128)(2,1)}, u32[]{:S(2)}) copy-start(bf16[2048,1,128]{2,1,0:T(2,128)(2,1)} %get-tuple-element.978) | copy-start | bytes 1572868
  175.7 20.1 %copy-start.3 = (bf16[2048,1,128]{0,2,1:T(8,128)(2,1)S(1)}, bf16[2048,1,128]{0,2,1:T(8,128)(2,1)}, u32[]{:S(2)}) copy-start(bf16[2048,1,128]{0,2,1:T(8,128)(2,1)} %get-tuple-element.982) | copy-start | bytes 1572868
Sparse Core Ops, SparseCore 0:
  8.9 22.2 all-gather.3
  36.0 40.0 all-gather.5
  78.3 40.6 all-gather.7
where the time goes:
time: 221 us; the launch traced here: 219 us
  waiting for transfers between devices  89 us (40%)
  matrix products  47.3 us (21%)
  local copies, waits for them, and re-layouts  28.9 us (13%)
  loops' own time  21.6 us (10%)
  other arithmetic  19.1 us (9%)
  between operations  13.5 us (6%)
    all_gather x1, waiting for transfers between devices, attend(): value_piece = lax.all_gather(values, 'ctx', axis=0, tiled=True)  39.1 us
    all_gather x1, waiting for transfers between devices, attend(): key_piece = lax.all_gather(keys, 'ctx', axis=0, tiled=True)  25.6 us
    all_gather x1, waiting for transfers between devices, local(): gathered = lax.all_gather(activations, 'tp', axis=0, tiled=True)  23.6 us
    another operation x4, loops' own time, per_query(): lax.scan(per_key, (row_top, totals, accum), (key_blocks, value_blocks, bl...  20.8 us
    dot_general x16, matrix products, block_update(): lax.dot_general(query_block, key_block, (((1,), (1,)), ((), ())), preferr...  16.5 us
    dot_general x16, matrix products, block_update(): jnp.dot(weights.astype(jnp.bfloat16), value_block, preferred_element_type...  15.7 us
    add x16, other arithmetic, per_key(): key_pos = key_start + jnp.arange(key_step, dtype=jnp.int32)  10.2 us
    dynamic_slice x16, local copies, waits for them, and re-layouts, per_query(): lax.scan(per_key, (row_top, totals, accum), (key_blocks, value_blocks, bl...  9.76 us
  transfers between devices with their start and end apart: 3, of which 3 were waited for; matrix products, arithmetic and copies ran while one was open for 8% of the time, Pallas kernels for 0%

commit v1 on v0

--- a/solution.py
+++ b/solution.py
@@ -61,8 +61,11 @@
             )
         )
     carry = tuple(carry_start)
-    key_piece = lax.all_gather(keys, "ctx", axis=0, tiled=True)
-    value_piece = lax.all_gather(values, "ctx", axis=0, tiled=True)
+    key_piece, value_piece = jnp.split(
+        lax.all_gather(jnp.concatenate([keys, values], axis=1), "ctx", axis=0, tiled=True),
+        [keys.shape[1]],
+        axis=1,
+    )
     piece_rows = key_piece.shape[0]
     key_step = math.gcd(piece_rows, 512)
     updated = []

time: 221 us -> 202 us (0.914)
  waiting for transfers between devices: 89 us -> 63.2 us
  local copies, waits for them, and re-layouts: 28.9 us -> 40.6 us
  matrix products: 47.3 us -> 42.5 us
    all_gather x2 -> x1, waiting for transfers between devices: 64.7 us -> 38.9 us  [attend(): lax.all_gather(jnp.concatenate([keys, values], axis=1), 'ctx', axis=0, ti...]
    dot_general x16, matrix products: 15.7 us -> 8.29 us  [block_update(): jnp.dot(weights.astype(jnp.bfloat16), value_block, preferred_element_type...]
    dynamic_slice x1, local copies, waits for them, and re-layouts: 2.71 us -> 7.93 us  [attend(): lax.dynamic_index_in_dim(key_piece.reshape(piece_rows, -1, HD), kv_slot,...]
    split x0 -> x1, local copies, waits for them, and re-layouts: none -> 4.49 us  [attend(): jnp.split(lax.all_gather(jnp.concatenate([keys, values], axis=1), 'ctx',...]
    reshape x0 -> x1, local copies, waits for them, and re-layouts: none -> 3.96 us  [attend(): key_piece.reshape(piece_rows, -1, HD)]
    dot_general x16, matrix products: 16.5 us -> 19.9 us  [block_update(): lax.dot_general(query_block, key_block, (((1,), (1,)), ((), ())), preferr...]
    unnamed x21 -> x16, local copies, waits for them, and re-layouts: 5.44 us -> 3.97 us
  transfers between devices with their start and end apart: 3 -> 2, of which waited for: 3 -> 2; matrix products, arithmetic and copies ran while one was open for 8% -> 5% of each run, Pallas kernels for 0% -> 0%
where the time goes in v1:
time: 202 us; the launch traced here: 201 us
  waiting for transfers between devices  63.2 us (31%)
  matrix products  42.5 us (21%)
  local copies, waits for them, and re-layouts  40.6 us (20%)
  loops' own time  20.7 us (10%)
  other arithmetic  19.8 us (10%)
  between operations  13.8 us (7%)
    all_gather x1, waiting for transfers between devices, attend(): lax.all_gather(jnp.concatenate([keys, values], axis=1), 'ctx', axis=0, ti...  38.9 us
    all_gather x1, waiting for transfers between devices, local(): gathered = lax.all_gather(activations, 'tp', axis=0, tiled=True)  23.6 us
    dot_general x16, matrix products, block_update(): lax.dot_general(query_block, key_block, (((1,), (1,)), ((), ())), preferr...  19.9 us
    another operation x4, loops' own time, per_query(): lax.scan(per_key, (row_top, totals, accum), (key_blocks, value_blocks, bl...  19.9 us
    add x16, other arithmetic, per_key(): key_pos = key_start + jnp.arange(key_step, dtype=jnp.int32)  10.4 us
    dynamic_slice x16, local copies, waits for them, and re-layouts, per_query(): lax.scan(per_key, (row_top, totals, accum), (key_blocks, value_blocks, bl...  10.1 us
    dot_general x16, matrix products, block_update(): jnp.dot(weights.astype(jnp.bfloat16), value_block, preferred_element_type...  8.29 us
    dot_general x1, matrix products, local(): jnp.dot(gathered, query_weight, preferred_element_type=jnp.float32)  8.09 us
  transfers between devices with their start and end apart: 2, of which 2 were waited for; matrix products, arithmetic and copies ran while one was open for 5% of the time, Pallas kernels for 0%

profile of v1, /device:TPU:25, one launch (start us, length us, event | category | flops | bytes accessed | tf_op | source)
XLA Modules:
  0.0 200.7 jit_solution(15837843334226116425)
XLA Ops:
  7.6 23.6 %all-gather.3.cloned.1.call-done = bf16[128,4096]{1,0:T(8,128)(2,1)} async-done(((bf16[64,4096]{1,0:T(8,128)(2,1)}), bf16[128,4096]{1,0:T(8,128)(2,1)}) %all-gather.3.cloned.1.call-update) | async-done | bytes 1048592 | tf_op jit(solution)/shard_map/all_gather | solution.py:130
  31.2 3.3 %fusion.79 = f32[128,512]{1,0:T(8,128)S(1)} fusion(bf16[128,4096]{1,0:T(8,128)(2,1)} %all-gather.3.cloned.1.call-done, bf16[4096,512]{1,0:T(8,128)(2,1)} %param.22), kind=kOutput, calls=%fused_computation.126 | convolution fusion | flops 536870912 | bytes 5505024 | tf_op jit(solution)/shard_map/dot_general | solution.py:134
  35.2 2.9 %convolution_convert_fusion = bf16[128,512]{1,0:T(8,128)(2,1)S(1)} fusion(bf16[128,4096]{1,0:T(8,128)(2,1)S(1)} %copy-done, bf16[4096,512]{1,0:T(8,128)(2,1)} %param.23), kind=kOutput, calls=%fused_computation.93 | convolution fusion | flops 536936448 | bytes 5373952 | tf_op jit(solution)/shard_map/dot_general | solution.py:135
  39.5 8.1 %convolution_bitcast_fusion = f32[16,8,16,128]{3,1,2,0:T(8,128)S(1)} fusion(bf16[128,4096]{1,0:T(8,128)(2,1)S(1)} %copy-done, bf16[4096,2048]{1,0:T(8,128)(2,1)} %param.21), kind=kOutput, calls=%fused_computation.92 | convolution fusion | flops 2147483648 | bytes 18874368 | tf_op jit(solution)/shard_map/dot_general | solution.py:133
  48.3 1.2 fusion.73
  49.5 38.9 %all-gather.5.cloned.1.call-done = bf16[2048,1024]{1,0:T(8,128)(2,1)} async-done(((bf16[128,1024]{1,0:T(8,128)(2,1)}), bf16[2048,1024]{1,0:T(8,128)(2,1)}) %all-gather.5.cloned.1.call-update) | async-done | bytes 4194320 | tf_op jit(solution)/shard_map/all_gather | solution.py:65
  88.5 4.5 %fusion.76 = (bf16[2048,512]{1,0:T(8,128)(2,1)}, bf16[2048,512]{1,0:T(8,128)(2,1)}) fusion(bf16[2048,1024]{1,0:T(8,128)(2,1)} %all-gather.5.cloned.1.call-done), kind=kLoop, calls=%fused_computation.123 | loop fusion | bytes 8388608 | tf_op jit(solution)/shard_map/split | solution.py:64
  93.0 2.5 %reshape.177 = bf16[2048,4,128]{2,1,0:T(4,128)(2,1)S(1)} reshape(bf16[2048,512]{1,0:T(8,128)(2,1)} %get-tuple-element.897) | data formatting | bytes 4194304 | tf_op jit(solution)/shard_map/reshape | solution.py:77
  95.5 4.0 %reshape.174 = bf16[2048,4,128]{2,1,0:T(4,128)(2,1)} reshape(bf16[2048,512]{1,0:T(8,128)(2,1)} %get-tuple-element.898) | data formatting | bytes 4194304 | tf_op jit(solution)/shard_map/reshape | solution.py:74
  99.5 7.9 %fusion.78 = (bf16[2048,1,128]{2,1,0:T(2,128)(2,1)S(1)}, bf16[2048,1,128]{2,1,0:T(2,128)(2,1)S(1)}, bf16[2048,1,128]{2,1,0:T(2,128)(2,1)S(1)}, bf16[2048,1,128]{2,1,0:T(2,128)(2,1)S(1)}) fusion(bf16[2048,4,128]{2,1,0:T(4,128)(2,1)} %reshape.174), kind=kLoop, calls=%fused_computation.125 | loop fusion | bytes 4194304 | tf_op jit(solution)/shard_map/jit(dynamic_index_in_dim)/dynamic_slice | solution.py:73
  108.3 0.9 copy.25
  110.9 4.0 %fusion.77 = (bf16[2048,1,128]{2,1,0:T(2,128)(2,1)S(1)}, bf16[2048,1,128]{2,1,0:T(2,128)(2,1)}, bf16[2048,1,128]{2,1,0:T(2,128)(2,1)}, bf16[2048,1,128]{2,1,0:T(2,128)(2,1)S(1)}) fusion(bf16[2048,4,128]{2,1,0:T(4,128)(2,1)S(1)} %reshape.177), kind=kLoop, calls=%fused_computation.124 | loop fusion | bytes 4194304 | tf_op jit(solution)/shard_map/jit(dynamic_index_in_dim)/dynamic_slice | solution.py:76
  115.0 19.1 %while.96 = (s32[]{:T(128)}, f32[512]{0:T(512)S(1)}, f32[512]{0:T(512)S(1)}, f32[512,128]{1,0:T(8,128)S(1)}, s32[4]{0:T(128)S(1)}, /*index=5*/s32[]{:T(128)}, bf...) while((s32[]{:T(128)}, f32[512]{0:T(512)S(1)}, ...), condition=%wide.region_6.7_spmd.clone, body=%wide.region_1.0_spmd.clone.sunk | while | flops 137496064 | bytes 4121887 | solution.py:103
  116.9 2.9 %conditional.12 = ((f32[512]{0:T(512)S(1)}, f32[512]{0:T(512)S(1)}, f32[512,128]{1,0:T(8,128)S(1)})) conditional(s32[]{:T(128)} %convert_element_type.119, (f32[512]{0:T(512)S(1)}, f32[512]{0:T(512)S(1)}, f32[512,128]{1,0:T(8,128)S(1)}) %tuple.156, (s32[]{:T(128)}, s32[512]{0:T(512)S(1)}, s32[128]{0:T(128)S(1)}, bf16[4,512,128]{2,1,0:T(8,128)(2,1)}, ...), branch_computations={%region_2.2_spmd, %region_3.5_spmd} | conditional | flops 137496064 | bytes 4119592 | solution.py:93
  117.7 1.3 fusion.9
  121.6 2.9 %conditional.12 = ((f32[512]{0:T(512)S(1)}, f32[512]{0:T(512)S(1)}, f32[512,128]{1,0:T(8,128)S(1)})) conditional(s32[]{:T(128)} %convert_element_type.119, (f32[512]{0:T(512)S(1)}, f32[512]{0:T(512)S(1)}, f32[512,128]{1,0:T(8,128)S(1)}) %tuple.156, (s32[]{:T(128)}, s32[512]{0:T(512)S(1)}, s32[128]{0:T(128)S(1)}, bf16[4,512,128]{2,1,0:T(8,128)(2,1)}, ...), branch_computations={%region_2.2_spmd, %region_3.5_spmd} | conditional | flops 137496064 | bytes 4119592 | solution.py:93
  122.5 1.3 fusion.9
  126.4 2.9 %conditional.12 = ((f32[512]{0:T(512)S(1)}, f32[512]{0:T(512)S(1)}, f32[512,128]{1,0:T(8,128)S(1)})) conditional(s32[]{:T(128)} %convert_element_type.119, (f32[512]{0:T(512)S(1)}, f32[512]{0:T(512)S(1)}, f32[512,128]{1,0:T(8,128)S(1)}) %tuple.156, (s32[]{:T(128)}, s32[512]{0:T(512)S(1)}, s32[128]{0:T(128)S(1)}, bf16[4,512,128]{2,1,0:T(8,128)(2,1)}, ...), branch_computations={%region_2.2_spmd, %region_3.5_spmd} | conditional | flops 137496064 | bytes 4119592 | solution.py:93
  127.3 1.3 fusion.9
  131.2 2.9 %conditional.12 = ((f32[512]{0:T(512)S(1)}, f32[512]{0:T(512)S(1)}, f32[512,128]{1,0:T(8,128)S(1)})) conditional(s32[]{:T(128)} %convert_element_type.119, (f32[512]{0:T(512)S(1)}, f32[512]{0:T(512)S(1)}, f32[512,128]{1,0:T(8,128)S(1)}) %tuple.156, (s32[]{:T(128)}, s32[512]{0:T(512)S(1)}, s32[128]{0:T(128)S(1)}, bf16[4,512,128]{2,1,0:T(8,128)(2,1)}, ...), branch_computations={%region_2.2_spmd, %region_3.5_spmd} | conditional | flops 137496064 | bytes 4119592 | solution.py:93
  132.1 1.3 fusion.9
  134.6 19.6 %while.98 = (s32[]{:T(128)}, f32[512]{0:T(512)S(1)}, f32[512]{0:T(512)S(1)}, f32[512,128]{1,0:T(8,128)S(1)}, s32[4]{0:T(128)S(1)}, /*index=5*/s32[]{:T(128)}, bf...) while((s32[]{:T(128)}, f32[512]{0:T(512)S(1)}, ...), condition=%wide.region_18.19_spmd.clone, body=%wide.region_13.18_spmd.clone.sunk | while | flops 137496064 | bytes 4121887 | solution.py:103
  136.5 2.9 %conditional.14 = ((f32[512]{0:T(512)S(1)}, f32[512]{0:T(512)S(1)}, f32[512,128]{1,0:T(8,128)S(1)})) conditional(s32[]{:T(128)} %convert_element_type.121, (f32[512]{0:T(512)S(1)}, f32[512]{0:T(512)S(1)}, f32[512,128]{1,0:T(8,128)S(1)}) %tuple.162, (s32[]{:T(128)}, s32[512]{0:T(512)S(1)}, s32[128]{0:T(128)S(1)}, bf16[4,512,128]{2,1,0:T(8,128)(2,1)}, ...), branch_computations={%region_14.14_spmd, %region_15.17_spmd} | conditional | flops 137496064 | bytes 4119592 | solution.py:93
  137.4 1.2 fusion.41
  141.4 2.9 %conditional.14 = ((f32[512]{0:T(512)S(1)}, f32[512]{0:T(512)S(1)}, f32[512,128]{1,0:T(8,128)S(1)})) conditional(s32[]{:T(128)} %convert_element_type.121, (f32[512]{0:T(512)S(1)}, f32[512]{0:T(512)S(1)}, f32[512,128]{1,0:T(8,128)S(1)}) %tuple.162, (s32[]{:T(128)}, s32[512]{0:T(512)S(1)}, s32[128]{0:T(128)S(1)}, bf16[4,512,128]{2,1,0:T(8,128)(2,1)}, ...), branch_computations={%region_14.14_spmd, %region_15.17_spmd} | conditional | flops 137496064 | bytes 4119592 | solution.py:93
  142.3 1.2 fusion.41
  146.3 2.9 %conditional.14 = ((f32[512]{0:T(512)S(1)}, f32[512]{0:T(512)S(1)}, f32[512,128]{1,0:T(8,128)S(1)})) conditional(s32[]{:T(128)} %convert_element_type.121, (f32[512]{0:T(512)S(1)}, f32[512]{0:T(512)S(1)}, f32[512,128]{1,0:T(8,128)S(1)}) %tuple.162, (s32[]{:T(128)}, s32[512]{0:T(512)S(1)}, s32[128]{0:T(128)S(1)}, bf16[4,512,128]{2,1,0:T(8,128)(2,1)}, ...), branch_computations={%region_14.14_spmd, %region_15.17_spmd} | conditional | flops 137496064 | bytes 4119592 | solution.py:93
  147.2 1.2 fusion.41
  151.2 2.9 %conditional.14 = ((f32[512]{0:T(512)S(1)}, f32[512]{0:T(512)S(1)}, f32[512,128]{1,0:T(8,128)S(1)})) conditional(s32[]{:T(128)} %convert_element_type.121, (f32[512]{0:T(512)S(1)}, f32[512]{0:T(512)S(1)}, f32[512,128]{1,0:T(8,128)S(1)}) %tuple.162, (s32[]{:T(128)}, s32[512]{0:T(512)S(1)}, s32[128]{0:T(128)S(1)}, bf16[4,512,128]{2,1,0:T(8,128)(2,1)}, ...), branch_computations={%region_14.14_spmd, %region_15.17_spmd} | conditional | flops 137496064 | bytes 4119592 | solution.py:93
  152.1 1.2 fusion.41
  154.6 18.9 %while.97 = (s32[]{:T(128)}, f32[512]{0:T(512)S(1)}, f32[512]{0:T(512)S(1)}, f32[512,128]{1,0:T(8,128)S(1)}, s32[4]{0:T(128)S(1)}, /*index=5*/s32[]{:T(128)}, bf...) while((s32[]{:T(128)}, f32[512]{0:T(512)S(1)}, ...), condition=%wide.region_12.13_spmd.clone, body=%wide.region_7.12_spmd.clone.sunk | while | flops 137496064 | bytes 4121887 | solution.py:103
  156.4 2.9 %conditional.13 = ((f32[512]{0:T(512)S(1)}, f32[512]{0:T(512)S(1)}, f32[512,128]{1,0:T(8,128)S(1)})) conditional(s32[]{:T(128)} %convert_element_type.120, (f32[512]{0:T(512)S(1)}, f32[512]{0:T(512)S(1)}, f32[512,128]{1,0:T(8,128)S(1)}) %tuple.159, (s32[]{:T(128)}, s32[512]{0:T(512)S(1)}, s32[128]{0:T(128)S(1)}, bf16[4,512,128]{2,1,0:T(8,128)(2,1)}, ...), branch_computations={%region_8.8_spmd, %region_9.11_spmd} | conditional | flops 137496064 | bytes 4119592 | solution.py:93
  157.2 1.2 fusion.25
  161.1 2.9 %conditional.13 = ((f32[512]{0:T(512)S(1)}, f32[512]{0:T(512)S(1)}, f32[512,128]{1,0:T(8,128)S(1)})) conditional(s32[]{:T(128)} %convert_element_type.120, (f32[512]{0:T(512)S(1)}, f32[512]{0:T(512)S(1)}, f32[512,128]{1,0:T(8,128)S(1)}) %tuple.159, (s32[]{:T(128)}, s32[512]{0:T(512)S(1)}, s32[128]{0:T(128)S(1)}, bf16[4,512,128]{2,1,0:T(8,128)(2,1)}, ...), branch_computations={%region_8.8_spmd, %region_9.11_spmd} | conditional | flops 137496064 | bytes 4119592 | solution.py:93
  162.0 1.2 fusion.25
  165.9 2.9 %conditional.13 = ((f32[512]{0:T(512)S(1)}, f32[512]{0:T(512)S(1)}, f32[512,128]{1,0:T(8,128)S(1)})) conditional(s32[]{:T(128)} %convert_element_type.120, (f32[512]{0:T(512)S(1)}, f32[512]{0:T(512)S(1)}, f32[512,128]{1,0:T(8,128)S(1)}) %tuple.159, (s32[]{:T(128)}, s32[512]{0:T(512)S(1)}, s32[128]{0:T(128)S(1)}, bf16[4,512,128]{2,1,0:T(8,128)(2,1)}, ...), branch_computations={%region_8.8_spmd, %region_9.11_spmd} | conditional | flops 137496064 | bytes 4119592 | solution.py:93
  166.7 1.2 fusion.25
  170.6 2.9 %conditional.13 = ((f32[512]{0:T(512)S(1)}, f32[512]{0:T(512)S(1)}, f32[512,128]{1,0:T(8,128)S(1)})) conditional(s32[]{:T(128)} %convert_element_type.120, (f32[512]{0:T(512)S(1)}, f32[512]{0:T(512)S(1)}, f32[512,128]{1,0:T(8,128)S(1)}) %tuple.159, (s32[]{:T(128)}, s32[512]{0:T(512)S(1)}, s32[128]{0:T(128)S(1)}, bf16[4,512,128]{2,1,0:T(8,128)(2,1)}, ...), branch_computations={%region_8.8_spmd, %region_9.11_spmd} | conditional | flops 137496064 | bytes 4119592 | solution.py:93
  171.4 1.2 fusion.25
  173.9 18.9 %while.99 = (s32[]{:T(128)}, f32[512]{0:T(512)S(1)}, f32[512]{0:T(512)S(1)}, f32[512,128]{1,0:T(8,128)S(1)}, s32[4]{0:T(128)S(1)}, /*index=5*/s32[]{:T(128)}, bf...) while((s32[]{:T(128)}, f32[512]{0:T(512)S(1)}, ...), condition=%wide.region_24.25_spmd.clone, body=%wide.region_19.24_spmd.clone.sunk | while | flops 137496064 | bytes 4121887 | solution.py:103
  175.7 2.9 %conditional.15 = ((f32[512]{0:T(512)S(1)}, f32[512]{0:T(512)S(1)}, f32[512,128]{1,0:T(8,128)S(1)})) conditional(s32[]{:T(128)} %convert_element_type.122, (f32[512]{0:T(512)S(1)}, f32[512]{0:T(512)S(1)}, f32[512,128]{1,0:T(8,128)S(1)}) %tuple.165, (s32[]{:T(128)}, s32[512]{0:T(512)S(1)}, s32[128]{0:T(128)S(1)}, bf16[4,512,128]{2,1,0:T(8,128)(2,1)}, ...), branch_computations={%region_20.20_spmd, %region_21.23_spmd} | conditional | flops 137496064 | bytes 4119592 | solution.py:93
  176.5 1.2 fusion.57
  180.4 2.9 %conditional.15 = ((f32[512]{0:T(512)S(1)}, f32[512]{0:T(512)S(1)}, f32[512,128]{1,0:T(8,128)S(1)})) conditional(s32[]{:T(128)} %convert_element_type.122, (f32[512]{0:T(512)S(1)}, f32[512]{0:T(512)S(1)}, f32[512,128]{1,0:T(8,128)S(1)}) %tuple.165, (s32[]{:T(128)}, s32[512]{0:T(512)S(1)}, s32[128]{0:T(128)S(1)}, bf16[4,512,128]{2,1,0:T(8,128)(2,1)}, ...), branch_computations={%region_20.20_spmd, %region_21.23_spmd} | conditional | flops 137496064 | bytes 4119592 | solution.py:93
  181.3 1.2 fusion.57
  185.1 2.9 %conditional.15 = ((f32[512]{0:T(512)S(1)}, f32[512]{0:T(512)S(1)}, f32[512,128]{1,0:T(8,128)S(1)})) conditional(s32[]{:T(128)} %convert_element_type.122, (f32[512]{0:T(512)S(1)}, f32[512]{0:T(512)S(1)}, f32[512,128]{1,0:T(8,128)S(1)}) %tuple.165, (s32[]{:T(128)}, s32[512]{0:T(512)S(1)}, s32[128]{0:T(128)S(1)}, bf16[4,512,128]{2,1,0:T(8,128)(2,1)}, ...), branch_computations={%region_20.20_spmd, %region_21.23_spmd} | conditional | flops 137496064 | bytes 4119592 | solution.py:93
  186.0 1.2 fusion.57
  189.9 2.9 %conditional.15 = ((f32[512]{0:T(512)S(1)}, f32[512]{0:T(512)S(1)}, f32[512,128]{1,0:T(8,128)S(1)})) conditional(s32[]{:T(128)} %convert_element_type.122, (f32[512]{0:T(512)S(1)}, f32[512]{0:T(512)S(1)}, f32[512,128]{1,0:T(8,128)S(1)}) %tuple.165, (s32[]{:T(128)}, s32[512]{0:T(512)S(1)}, s32[128]{0:T(128)S(1)}, bf16[4,512,128]{2,1,0:T(8,128)(2,1)}, ...), branch_computations={%region_20.20_spmd, %region_21.23_spmd} | conditional | flops 137496064 | bytes 4119592 | solution.py:93
  190.7 1.2 fusion.57
  (210 shorter events, 44.5 us)
Async XLA Ops:
  6.5 24.7 %all-gather.3.cloned.1.call-start = ((), (), s32[]{:S(2)}) async-start(), calls=%async_computation | async-start | bytes 1572864 | tf_op jit(solution)/shard_map/all_gather | solution.py:130
  7.3 81.2 %all-gather.5.cloned.1.call-start = ((), (), s32[]{:S(2)}) async-start(), calls=%async_computation.1 | async-start | bytes 4456448 | tf_op jit(solution)/shard_map/all_gather | solution.py:65
  31.2 3.9 %copy-start = (bf16[128,4096]{1,0:T(8,128)(2,1)S(1)}, bf16[128,4096]{1,0:T(8,128)(2,1)}, u32[]{:S(2)}) copy-start(bf16[128,4096]{1,0:T(8,128)(2,1)} %all-gather.3.cloned.1.call-done) | copy-start | bytes 3145732
  115.0 19.4 %copy-start.2 = (bf16[2048,1,128]{2,1,0:T(2,128)(2,1)S(1)}, bf16[2048,1,128]{2,1,0:T(2,128)(2,1)}, u32[]{:S(2)}) copy-start(bf16[2048,1,128]{2,1,0:T(2,128)(2,1)} %get-tuple-element.900) | copy-start | bytes 1572868
  134.6 19.9 %copy-start.1 = (bf16[2048,1,128]{2,1,0:T(2,128)(2,1)S(1)}, bf16[2048,1,128]{2,1,0:T(2,128)(2,1)}, u32[]{:S(2)}) copy-start(bf16[2048,1,128]{2,1,0:T(2,128)(2,1)} %get-tuple-element.901) | copy-start | bytes 1572868
Sparse Core Ops, SparseCore 0:
  8.9 22.2 all-gather.2
  38.9 49.4 all-gather.4
